TPU v7x, 32 devices: a whole 2x2x4 slice. The times are simulated.
32 devices in a mesh: vec: 4 (over z), row: 8 (over y, x, core).
Axes of the slice: x: 2, y: 2, z: 4, core: 2. Of those that a mesh axis runs over, the one named last changes fastest.
Arguments:
- chol_vectors: float32 [128, 1024, 1024], P('vec', 'row'), may hold values from -16 to 16, as said below
Outputs:
- rotated: float32 [128, 1024, 1024], P('vec', 'row')
- rotation: float32 [1024, 1024], P('row')
Inputs may be any that keep to these rules, and one draw needn't show every extreme that they name: Every matrix chol_vectors[P] is symmetric in its last two dimensions.
All inputs are finite; a program needn't handle non-finite values.
Results may differ from a plain program's by a relative error of at most 0.00014.
Values sent between devices are 32-bit elements; how exact they have to be, the bound alone decides.
No kernel may reach another device: no remote copies, remote signals or barrier semaphores. Data moves between devices by JAX's collectives and lax.ppermute only.
A program may use at most 128 MiB of HBM per device.

v0:
```python
import jax
import jax.numpy as jnp
from jax import lax
from jax.sharding import PartitionSpec as P

ITERS = 2
step_gain = 0.2


def shards(chol_vectors):
    row_count = chol_vectors.shape[1]
    orbitals = chol_vectors.shape[2]
    offset = lax.axis_index("row") * row_count
    highest = lax.Precision.HIGHEST
    local_rows = lax.broadcasted_iota(jnp.int32, (row_count, orbitals), 0) + offset
    local_cols = lax.broadcasted_iota(jnp.int32, (row_count, orbitals), 1)
    identity_rows = (local_rows == local_cols).astype(jnp.float32)
    current = chol_vectors
    rotation = identity_rows
    for iteration in range(ITERS):
        block = lax.dynamic_slice_in_dim(current, offset, row_count, 2)
        diagonal = jnp.diagonal(block, axis1=1, axis2=2)
        own_part = jnp.einsum("pjk,pj->jk", current, diagonal, precision=highest)
        diagonal_all = lax.all_gather(diagonal, "row", axis=1, tiled=True)
        other_part = jnp.einsum("pjk,pk->jk", current, diagonal_all, precision=highest)
        gradient = lax.psum(own_part - other_part, "vec")
        squares = lax.psum(jnp.sum(gradient * gradient), "row")
        norm = jnp.sqrt(squares / (orbitals * orbitals) + 1e-06)
        generator = step_gain / jnp.sqrt(jnp.float32(orbitals)) * gradient / norm
        generator_full = lax.all_gather(generator, "row", axis=0, tiled=True)
        identity_full = jnp.eye(orbitals, dtype=jnp.float32)
        step_full = (
            identity_full
            + generator_full
            + 0.5 * jnp.dot(generator_full, generator_full, precision=highest)
        )
        step_local = lax.dynamic_slice_in_dim(step_full, offset, row_count, 0)
        if iteration == 0:
            rotation = step_local
        else:
            rotation = jnp.dot(rotation, step_full, precision=highest)
        product_left = jnp.einsum("pjk,kl->pjl", current, step_full, precision=highest)
        columns = lax.all_to_all(product_left, "row", split_axis=2, concat_axis=1, tiled=True)
        current = jnp.einsum("pim,ik->pmk", columns, step_full, precision=highest)
    return (current, rotation)


def solution(mesh):
    placed = (P("vec", "row", None),)
    return jax.shard_map(
        shards,
        mesh=mesh,
        in_specs=placed,
        out_specs=(P("vec", "row", None), P("row", None)),
        check_vma=False,
    )
```

profile of v0, /device:TPU:0, one launch (start us, length us, event | category | flops | bytes accessed | tf_op | source)
XLA Modules:
  0.0 1111.6 jit_solution(9601472853553550261)
XLA Ops:
  7.2 0.0 all-reduce.3.cloned.1.call-start
  7.2 1.7 constant_dynamic-slice_fusion.1
  9.0 4.7 copy.37
  13.6 1.9 gather_fusion
  15.5 11.3 %all_gather.12 = f32[32,1024]{0,1:T(8,128)S(1)} all-gather(f32[32,128]{0,1:T(8,128)S(1)} %bitcast.73), channel_id=1, replica_groups=mesh['vec'=4,'row'=8] {'row'}, dimensions={1}, use_global_device_ids=true | all-gather | bytes 147456 | tf_op jit(solution)/shard_map/all_gather | solution.py:24
  26.8 0.2 copy.38
  27.0 8.4 multiply_reduce_fusion.1
  35.4 22.4 %fusion.2 = f32[128,1,1024]{2,1,0:T(1,128)S(1)} fusion(f32[32,128,1]{0,2,1:T(1,128)S(1)} %bitcast.74, f32[32,128,1024]{2,1,0:T(8,128)} %param.1), kind=kOutput, calls=%fused_computation.6 | convolution fusion | flops 50331648 | bytes 17317888 | tf_op jit(solution)/shard_map/pjk,pj->jk/dot_general | solution.py:23
  57.7 0.9 bitcast_subtract_fusion.1
  58.7 0.0 all-reduce.3.cloned.1.call-update
  58.7 0.0 all-gather.3.cloned.1.call-start
  58.7 38.9 %all-reduce.3.cloned.1.call-done = f32[128,1024]{1,0:T(8,128)} async-done(((f32[128,1024]{1,0:T(8,128)}), f32[128,1024]{1,0:T(8,128)}) %all-reduce.3.cloned.1.call-update) | async-done | bytes 524304 | tf_op jit(solution)/shard_map/psum | solution.py:26
  97.6 1.8 multiply_reduce_fusion.3
  99.4 13.3 %psum.29 = f32[]{:T(128)} all-reduce(f32[]{:T(128)} %multiply_reduce_fusion.3), channel_id=1, replica_groups=mesh['vec'=4,'row'=8] {'row'}, use_global_device_ids=true, to_apply=%region_2.3 | all-reduce | flops 1 | bytes 8 | tf_op jit(solution)/shard_map/psum | solution.py:27
  113.5 1.9 multiply_divide_fusion.1
  115.4 0.0 all-gather.3.cloned.1.call-update
  115.4 0.2 all-reduce.5.cloned.1.call-start
  115.6 34.5 %all-gather.3.cloned.1.call-done = f32[1024,1024]{1,0:T(8,128)} async-done(((f32[128,1024]{1,0:T(8,128)}), f32[1024,1024]{1,0:T(8,128)}) %all-gather.3.cloned.1.call-update) | async-done | bytes 4194320 | tf_op jit(solution)/shard_map/all_gather | solution.py:30
  150.1 18.2 %fusion.4 = f32[1024,1024]{1,0:T(8,128)S(1)} fusion(f32[1024,1024]{1,0:T(8,128)} %all-gather.3.cloned.1.call-done), kind=kOutput, calls=%fused_computation.13 | convolution fusion | flops 12890144768 | bytes 8388608 | tf_op jit(solution)/shard_map/dot_general | solution.py:35
  168.3 0.0 copy-start.2
  168.3 1.9 copy-done.2
  170.2 109.4 %convolution_bitcast_fusion = f32[32,128,1024]{1,2,0:T(8,128)} fusion(f32[32,128,1024]{2,1,0:T(8,128)} %param.1, f32[1024,1024]{1,0:T(8,128)S(1)} %fusion.4), kind=kOutput, calls=%fused_computation.10 | convolution fusion | flops 51539607552 | bytes 37748736 | tf_op jit(solution)/shard_map/pjk,kl->pjl/dot_general | solution.py:42
  279.7 15.2 %copy.10 = f32[32,128,1024]{1,0,2:T(8,128)S(1)} copy(f32[32,128,1024]{1,2,0:T(8,128)} %convolution_bitcast_fusion) | data formatting | bytes 33554432 | tf_op jit(solution)/shard_map/pjk,kl->pjl/dot_general | solution.py:42
  294.9 186.6 %all_to_all.36 = f32[32,128,1024]{1,0,2:T(8,128)S(1)} all-to-all(f32[32,128,1024]{1,0,2:T(8,128)S(1)} %copy.10), channel_id=1, replica_groups=mesh['vec'=4,'row'=8] {'row'}, dimensions={2} | all-to-all | bytes 33554432 | tf_op jit(solution)/shard_map/all_to_all | solution.py:43
  481.5 19.3 %copy.51 = f32[32,128,8,128]{1,2,3,0:T(8,128)} copy(f32[32,128,8,128]{1,0,3,2:T(8,128)S(1)} %bitcast.66) | data formatting | bytes 33554432 | tf_op jit(solution)/shard_map/all_to_all | solution.py:43
  500.9 18.0 %all_to_all.29 = f32[32,1024,128]{1,2,0:T(8,128)} reshape(f32[32,8,128,128]{2,1,3,0:T(8,128)} %bitcast.67) | data formatting | bytes 33554432 | tf_op jit(solution)/shard_map/all_to_all | solution.py:43
  518.9 57.9 %fusion.10 = f32[32,128,1024]{2,1,0:T(8,128)S(1)} fusion(f32[32,1024,128]{1,2,0:T(8,128)} %all_to_all.29, f32[1024,1024]{1,0:T(8,128)} %copy-done.2), kind=kOutput, calls=%fused_computation.19 | convolution fusion | flops 51539607552 | bytes 37748736 | tf_op jit(solution)/shard_map/pim,ik->pmk/dot_general | solution.py:44
  576.8 0.0 copy-start
  576.8 6.2 copy-done
  582.9 0.3 constant_dynamic-slice_fusion
  583.2 4.7 copy.12
  587.9 1.8 gather_fusion.1
  589.7 8.9 all_gather.14
  598.6 0.2 copy.39
  598.8 8.3 multiply_reduce_fusion
  607.1 22.2 %fusion = f32[128,1,1024]{2,1,0:T(1,128)S(1)} fusion(f32[32,128,1]{0,2,1:T(1,128)S(1)} %bitcast.72, f32[32,128,1024]{2,1,0:T(8,128)} %copy-done), kind=kOutput, calls=%fused_computation.3 | convolution fusion | flops 50331648 | bytes 17317888 | tf_op jit(solution)/shard_map/pjk,pj->jk/dot_general | solution.py:23
  629.3 0.9 bitcast_subtract_fusion
  630.2 0.0 all-reduce.5.cloned.1.call-update
  630.3 0.0 all-gather.5.cloned.1.call-start
  630.3 38.8 %all-reduce.5.cloned.1.call-done = f32[128,1024]{1,0:T(8,128)} async-done(((f32[128,1024]{1,0:T(8,128)}), f32[128,1024]{1,0:T(8,128)}) %all-reduce.5.cloned.1.call-update) | async-done | bytes 524304 | tf_op jit(solution)/shard_map/psum | solution.py:26
  669.1 1.8 multiply_reduce_fusion.2
  670.9 13.3 %psum.31 = f32[]{:T(128)} all-reduce(f32[]{:T(128)} %multiply_reduce_fusion.2), channel_id=1, replica_groups=mesh['vec'=4,'row'=8] {'row'}, use_global_device_ids=true, to_apply=%region_5.6 | all-reduce | flops 1 | bytes 8 | tf_op jit(solution)/shard_map/psum | solution.py:27
  684.9 1.9 multiply_divide_fusion
  686.8 0.0 all-gather.5.cloned.1.call-update
  686.8 34.7 %all-gather.5.cloned.1.call-done = f32[1024,1024]{1,0:T(8,128)} async-done(((f32[128,1024]{1,0:T(8,128)}), f32[1024,1024]{1,0:T(8,128)}) %all-gather.5.cloned.1.call-update) | async-done | bytes 4194320 | tf_op jit(solution)/shard_map/all_gather | solution.py:30
  721.6 18.2 %fusion.5 = f32[1024,1024]{1,0:T(8,128)S(1)} fusion(f32[1024,1024]{1,0:T(8,128)} %all-gather.5.cloned.1.call-done), kind=kOutput, calls=%fused_computation.14 | convolution fusion | flops 12890144768 | bytes 8388608 | tf_op jit(solution)/shard_map/dot_general | solution.py:35
  739.8 0.0 copy-start.1
  739.8 2.0 copy-done.1
  741.7 58.7 %fusion.8 = f32[32,128,1024]{2,1,0:T(8,128)} fusion(f32[32,128,1024]{2,1,0:T(8,128)} %copy-done, f32[1024,1024]{1,0:T(8,128)S(1)} %fusion.5), kind=kOutput, calls=%fused_computation.17 | convolution fusion | flops 51539607552 | bytes 37748736 | tf_op jit(solution)/shard_map/pjk,kl->pjl/dot_general | solution.py:42
  800.5 17.4 %copy.13 = f32[32,128,1024]{1,0,2:T(8,128)} copy(f32[32,128,1024]{2,1,0:T(8,128)} %fusion.8) | data formatting | bytes 33554432 | tf_op jit(solution)/shard_map/pjk,kl->pjl/dot_general | solution.py:42
  817.8 5.9 all-to-all-start.1
  823.8 5.6 fusion.13
  829.3 178.2 %all-to-all-done.1 = f32[32,128,1024]{1,0,2:T(8,128)} async-done(((f32[32,128,1024]{1,0,2:T(8,128)}), f32[32,128,1024]{1,0,2:T(8,128)}, u32[]{:S(2)}, u32[]{:S(2)}) %all-to-all-start.1) | async-done | bytes 16777248 | tf_op jit(solution)/shard_map/all_to_all | solution.py:43
  1007.5 17.8 %copy.50 = f32[32,128,8,128]{1,2,3,0:T(8,128)} copy(f32[32,128,8,128]{1,0,3,2:T(8,128)} %bitcast.21) | data formatting | bytes 33554432 | tf_op jit(solution)/shard_map/all_to_all | solution.py:43
  1025.3 18.0 %all_to_all.33 = f32[32,1024,128]{1,2,0:T(8,128)} reshape(f32[32,8,128,128]{2,1,3,0:T(8,128)} %bitcast.68) | data formatting | bytes 33554432 | tf_op jit(solution)/shard_map/all_to_all | solution.py:43
  1043.3 61.6 %fusion.6 = f32[32,128,1024]{2,1,0:T(8,128)} fusion(f32[32,1024,128]{1,2,0:T(8,128)} %all_to_all.33, f32[1024,1024]{1,0:T(8,128)} %copy-done.1), kind=kOutput, calls=%fused_computation.15 | convolution fusion | flops 51539607552 | bytes 37748736 | tf_op jit(solution)/shard_map/pim,ik->pmk/dot_general | solution.py:44
  (1 shorter events, 0.0 us)
Async XLA Ops:
  7.2 90.5 %all-reduce.3.cloned.1.call-start = ((), (), s32[]{:S(2)}) async-start(), calls=%async_computation.2 | async-start | bytes 1048576 | tf_op jit(solution)/shard_map/psum | solution.py:26
  58.7 91.4 %all-gather.3.cloned.1.call-start = ((), (), s32[]{:S(2)}) async-start(), calls=%async_computation.3 | async-start | bytes 4718592 | tf_op jit(solution)/shard_map/all_gather | solution.py:30
  115.4 553.7 %all-reduce.5.cloned.1.call-start = ((), (), s32[]{:S(2)}) async-start(), calls=%async_computation.4 | async-start | bytes 1048576 | tf_op jit(solution)/shard_map/psum | solution.py:26
  168.3 1.9 copy-start.2
  576.8 6.2 copy-start
  630.3 91.3 %all-gather.5.cloned.1.call-start = ((), (), s32[]{:S(2)}) async-start(), calls=%async_computation.5 | async-start | bytes 4718592 | tf_op jit(solution)/shard_map/all_gather | solution.py:30
  739.8 2.0 copy-start.1
  817.8 189.7 %all-to-all-start.1 = ((f32[32,128,1024]{1,0,2:T(8,128)}), f32[32,128,1024]{1,0,2:T(8,128)}, u32[]{:S(2)}, u32[]{:S(2)}) async-start(f32[32,128,1024]{1,0,2:T(8,128)} %copy.13), calls=%async_computation.1 | async-start | bytes 33554432 | tf_op jit(solution)/shard_map/all_to_all | solution.py:43
Sparse Core Ops, SparseCore 0:
  58.8 38.7 all-reduce.2
  115.5 34.5 all-gather.2
  630.4 38.6 all-reduce.4
  686.9 34.5 all-gather.4
where the time goes:
time: 1120 us; the launch traced here: 1110 us
  matrix products  374 us (33%)
  waiting for transfers between devices  325 us (29%)
  blocking collectives  234 us (21%)
  local copies, waits for them, and re-layouts  131 us (12%)
  other arithmetic  25.9 us (2%)
  between operations  15.5 us (1%)
    all_to_all x1, blocking collectives, shards(): lax.all_to_all(product_left, 'row', split_axis=2, concat_axis=1, tiled=True)  187 us
    all_to_all x1, waiting for transfers between devices, shards(): lax.all_to_all(product_left, 'row', split_axis=2, concat_axis=1, tiled=True)  178 us
    dot_general x2, matrix products, shards(): jnp.einsum('pjk,kl->pjl', current, step_full, precision=highest)  168 us
    dot_general x2, matrix products, shards(): current = jnp.einsum('pim,ik->pmk', columns, step_full, precision=highest)  120 us
    psum x2, waiting for transfers between devices, shards(): gradient = lax.psum(own_part - other_part, 'vec')  77.7 us
    all_to_all x4, local copies, waits for them, and re-layouts, shards(): lax.all_to_all(product_left, 'row', split_axis=2, concat_axis=1, tiled=True)  73.1 us
    all_gather x2, waiting for transfers between devices, shards(): generator_full = lax.all_gather(generator, 'row', axis=0, tiled=True)  69.3 us
    dot_general x2, matrix products, shards(): own_part = jnp.einsum('pjk,pj->jk', current, diagonal, precision=highest)  44.6 us
  transfers between devices with their start and end apart: 5, of which 5 were waited for; matrix products, arithmetic and copies ran while one was open for 0% of the time, Pallas kernels for 0%

commit v1 on v0

--- a/solution.py
+++ b/solution.py
@@ -40,7 +40,12 @@
         else:
             rotation = jnp.dot(rotation, step_full, precision=highest)
         product_left = jnp.einsum("pjk,kl->pjl", current, step_full, precision=highest)
-        columns = lax.all_to_all(product_left, "row", split_axis=2, concat_axis=1, tiled=True)
+        columns = jnp.concatenate(
+            jax.lax.all_to_all(
+                jnp.stack(jnp.split(product_left, jax.lax.axis_size("row"), axis=2)), "row", 0, 0
+            ),
+            axis=1,
+        )
         current = jnp.einsum("pim,ik->pmk", columns, step_full, precision=highest)
     return (current, rotation)
 

time: 1120 us -> 1060 us (0.946)
  local copies, waits for them, and re-layouts: 131 us -> 60.2 us
  matrix products: 374 us -> 387 us
    all_to_all x4 -> x0, local copies, waits for them, and re-layouts: 73.1 us -> none  [shards(): lax.all_to_all(product_left, 'row', split_axis=2, concat_axis=1, tiled=True)]
    dot_general x2 -> x0, local copies, waits for them, and re-layouts: 32.6 us -> none  [shards(): jnp.einsum('pjk,kl->pjl', current, step_full, precision=highest)]
    reshape x0 -> x2, local copies, waits for them, and re-layouts: none -> 24.6 us  [shards(): jnp.concatenate(jax.lax.all_to_all(jnp.stack(jnp.split(product_left, jax....]
    unnamed x9 -> x25, local copies, waits for them, and re-layouts: 15 us -> 23.5 us
  transfers between devices with their start and end apart: 5 -> 5, of which waited for: 5 -> 5; matrix products, arithmetic and copies ran while one was open for 0% -> 1% of each run, Pallas kernels for 0% -> 0%
where the time goes in v1:
time: 1060 us
  matrix products  387 us (37%)
  waiting for transfers between devices  325 us (31%)
  blocking collectives  235 us (22%)
  local copies, waits for them, and re-layouts  60.2 us (6%)
  other arithmetic  26.2 us (2%)
  between operations  15.8 us (1%)
    all_to_all x1, blocking collectives, shards(): jax.lax.all_to_all(jnp.stack(jnp.split(product_left, jax.lax.axis_size('r...  188 us
    all_to_all x1, waiting for transfers between devices, shards(): jax.lax.all_to_all(jnp.stack(jnp.split(product_left, jax.lax.axis_size('r...  178 us
    dot_general x2, matrix products, shards(): jnp.einsum('pjk,kl->pjl', current, step_full, precision=highest)  172 us
    dot_general x2, matrix products, shards(): current = jnp.einsum('pim,ik->pmk', columns, step_full, precision=highest)  129 us
    psum x2, waiting for transfers between devices, shards(): gradient = lax.psum(own_part - other_part, 'vec')  77.7 us
    all_gather x2, waiting for transfers between devices, shards(): generator_full = lax.all_gather(generator, 'row', axis=0, tiled=True)  69.2 us
    dot_general x2, matrix products, shards(): own_part = jnp.einsum('pjk,pj->jk', current, diagonal, precision=highest)  44.6 us
    dot_general x2, matrix products, shards(): jnp.dot(generator_full, generator_full, precision=highest)  36.5 us
  transfers between devices with their start and end apart: 5, of which 5 were waited for; matrix products, arithmetic and copies ran while one was open for 1% of the time, Pallas kernels for 0%

profile of v1, /device:TPU:0, one launch (start us, length us, event | category | flops | bytes accessed | tf_op | source)
XLA Modules:
  0.0 1055.6 jit_solution(4926335506419598859)
XLA Ops:
  7.2 0.0 all-reduce.3.cloned.1.call-start
  7.2 1.7 constant_dynamic-slice_fusion.1
  9.0 4.7 copy.37
  13.6 1.9 gather_fusion
  15.5 11.3 %all_gather.12 = f32[32,1024]{0,1:T(8,128)S(1)} all-gather(f32[32,128]{0,1:T(8,128)S(1)} %bitcast.125), channel_id=1, replica_groups=mesh['vec'=4,'row'=8] {'row'}, dimensions={1}, use_global_device_ids=true | all-gather | bytes 147456 | tf_op jit(solution)/shard_map/all_gather | solution.py:24
  26.8 0.2 copy.38
  27.0 8.5 multiply_reduce_fusion.1
  35.5 22.4 %fusion.2 = f32[128,1,1024]{2,1,0:T(1,128)S(1)} fusion(f32[32,128,1]{0,2,1:T(1,128)S(1)} %bitcast.126, f32[32,128,1024]{2,1,0:T(8,128)} %param.1), kind=kOutput, calls=%fused_computation.6 | convolution fusion | flops 50331648 | bytes 17317888 | tf_op jit(solution)/shard_map/pjk,pj->jk/dot_general | solution.py:23
  57.9 0.9 bitcast_subtract_fusion.1
  58.8 0.0 all-reduce.3.cloned.1.call-update
  58.8 0.0 all-gather.3.cloned.1.call-start
  58.9 38.9 %all-reduce.3.cloned.1.call-done = f32[128,1024]{1,0:T(8,128)} async-done(((f32[128,1024]{1,0:T(8,128)}), f32[128,1024]{1,0:T(8,128)}) %all-reduce.3.cloned.1.call-update) | async-done | bytes 524304 | tf_op jit(solution)/shard_map/psum | solution.py:26
  97.8 1.8 multiply_reduce_fusion.3
  99.5 13.3 %psum.29 = f32[]{:T(128)} all-reduce(f32[]{:T(128)} %multiply_reduce_fusion.3), channel_id=1, replica_groups=mesh['vec'=4,'row'=8] {'row'}, use_global_device_ids=true, to_apply=%region_2.3 | all-reduce | flops 1 | bytes 8 | tf_op jit(solution)/shard_map/psum | solution.py:27
  113.6 1.9 multiply_divide_fusion.1
  115.5 0.0 all-gather.3.cloned.1.call-update
  115.5 0.3 all-reduce.5.cloned.1.call-start
  115.8 34.4 %all-gather.3.cloned.1.call-done = f32[1024,1024]{1,0:T(8,128)} async-done(((f32[128,1024]{1,0:T(8,128)}), f32[1024,1024]{1,0:T(8,128)}) %all-gather.3.cloned.1.call-update) | async-done | bytes 4194320 | tf_op jit(solution)/shard_map/all_gather | solution.py:30
  150.2 18.3 %fusion.4 = f32[1024,1024]{1,0:T(8,128)S(1)} fusion(f32[1024,1024]{1,0:T(8,128)} %all-gather.3.cloned.1.call-done), kind=kOutput, calls=%fused_computation.11 | convolution fusion | flops 12890144768 | bytes 8388608 | tf_op jit(solution)/shard_map/dot_general | solution.py:35
  168.5 112.5 %convolution_bitcast_fusion = f32[32,128,1024]{1,2,0:T(8,128)S(1)} fusion(f32[32,128,1024]{2,1,0:T(8,128)} %param.1, f32[1024,1024]{1,0:T(8,128)S(1)} %fusion.4), kind=kOutput, calls=%fused_computation.8 | convolution fusion | flops 51539607552 | bytes 37748736 | tf_op jit(solution)/shard_map/pjk,kl->pjl/dot_general | solution.py:42
  281.0 0.1 fusion.28
  281.2 0.1 fusion.27
  281.3 0.1 fusion.26
  281.5 0.1 fusion.25
  281.6 0.1 fusion.24
  281.8 0.1 fusion.23
  281.9 0.1 fusion.22
  282.1 0.1 fusion.21
  282.2 187.7 %all_to_all.10 = f32[8,32,128,128]{2,3,1,0:T(8,128)} all-to-all(f32[8,32,128,128]{2,3,1,0:T(8,128)S(1)} %fusion.21), channel_id=1, replica_groups=mesh['vec'=4,'row'=8] {'row'}, dimensions={0} | all-to-all | bytes 33554432 | tf_op jit(solution)/shard_map/all_to_all | solution.py:44
  469.9 17.5 %copy.8 = f32[32,8,128,128]{3,2,1,0:T(8,128)} copy(f32[32,8,128,128]{2,3,0,1:T(8,128)} %bitcast.118) | data formatting | bytes 33554432 | tf_op jit(solution)/shard_map/reshape | solution.py:43
  487.4 71.4 %fusion.10 = f32[32,128,1024]{2,1,0:T(8,128)S(1)} fusion(f32[32,1024,128]{2,1,0:T(8,128)} %bitcast.120, f32[1024,1024]{1,0:T(8,128)} %copy-done.3), kind=kOutput, calls=%fused_computation.17 | convolution fusion | flops 51539607552 | bytes 37748736 | tf_op jit(solution)/shard_map/pim,ik->pmk/dot_general | solution.py:49
  558.7 0.0 copy-start
  558.7 6.2 copy-done
  564.9 0.3 constant_dynamic-slice_fusion
  565.2 4.7 copy.10
  569.9 1.8 gather_fusion.1
  571.7 8.9 all_gather.14
  580.6 0.2 copy.39
  580.7 8.5 multiply_reduce_fusion
  589.2 22.2 %fusion = f32[128,1,1024]{2,1,0:T(1,128)S(1)} fusion(f32[32,128,1]{0,2,1:T(1,128)S(1)} %bitcast.124, f32[32,128,1024]{2,1,0:T(8,128)} %copy-done), kind=kOutput, calls=%fused_computation.3 | convolution fusion | flops 50331648 | bytes 17317888 | tf_op jit(solution)/shard_map/pjk,pj->jk/dot_general | solution.py:23
  611.5 0.9 bitcast_subtract_fusion
  612.4 0.0 all-reduce.5.cloned.1.call-update
  612.4 0.0 all-gather.5.cloned.1.call-start
  612.5 38.8 %all-reduce.5.cloned.1.call-done = f32[128,1024]{1,0:T(8,128)} async-done(((f32[128,1024]{1,0:T(8,128)}), f32[128,1024]{1,0:T(8,128)}) %all-reduce.5.cloned.1.call-update) | async-done | bytes 524304 | tf_op jit(solution)/shard_map/psum | solution.py:26
  651.2 1.8 multiply_reduce_fusion.2
  653.0 13.3 %psum.31 = f32[]{:T(128)} all-reduce(f32[]{:T(128)} %multiply_reduce_fusion.2), channel_id=1, replica_groups=mesh['vec'=4,'row'=8] {'row'}, use_global_device_ids=true, to_apply=%region_5.6 | all-reduce | flops 1 | bytes 8 | tf_op jit(solution)/shard_map/psum | solution.py:27
  667.0 1.9 multiply_divide_fusion
  668.9 0.0 all-gather.5.cloned.1.call-update
  669.0 34.7 %all-gather.5.cloned.1.call-done = f32[1024,1024]{1,0:T(8,128)} async-done(((f32[128,1024]{1,0:T(8,128)}), f32[1024,1024]{1,0:T(8,128)}) %all-gather.5.cloned.1.call-update) | async-done | bytes 4194320 | tf_op jit(solution)/shard_map/all_gather | solution.py:30
  703.7 18.3 %fusion.5 = f32[1024,1024]{1,0:T(8,128)S(1)} fusion(f32[1024,1024]{1,0:T(8,128)} %all-gather.5.cloned.1.call-done), kind=kOutput, calls=%fused_computation.12 | convolution fusion | flops 12890144768 | bytes 8388608 | tf_op jit(solution)/shard_map/dot_general | solution.py:35
  722.0 59.2 %fusion.8 = f32[32,128,1024]{2,1,0:T(8,128)S(1)} fusion(f32[32,128,1024]{2,1,0:T(8,128)} %copy-done, f32[1024,1024]{1,0:T(8,128)S(1)} %fusion.5), kind=kOutput, calls=%fused_computation.15 | convolution fusion | flops 51539607552 | bytes 37748736 | tf_op jit(solution)/shard_map/pjk,kl->pjl/dot_general | solution.py:42
  781.2 1.6 fusion.20
  782.8 1.6 fusion.19
  784.5 1.6 fusion.18
  786.1 1.6 fusion.17
  787.7 1.6 fusion.16
  789.3 1.6 fusion.15
  790.9 1.6 fusion.14
  792.6 1.6 fusion.13
  794.2 5.8 all-to-all-start.1
  799.9 5.6 fusion.29
  805.5 178.4 %all-to-all-done.1 = f32[8,32,128,128]{3,2,1,0:T(8,128)} async-done(((f32[8,32,128,128]{3,2,1,0:T(8,128)}), f32[8,32,128,128]{3,2,1,0:T(8,128)}, u32[]{:S(2)}, u32[]{:S(2)}) %all-to-all-start.1) | async-done | bytes 16777248 | tf_op jit(solution)/shard_map/all_to_all | solution.py:44
  983.9 7.1 copy.11
  991.0 57.7 %fusion.6 = f32[32,128,1024]{2,1,0:T(8,128)} fusion(f32[32,1024,128]{2,1,0:T(8,128)S(1)} %bitcast.119, f32[1024,1024]{1,0:T(8,128)S(1)} %copy-done.2), kind=kOutput, calls=%fused_computation.13 | convolution fusion | flops 51539607552 | bytes 37748736 | tf_op jit(solution)/shard_map/pim,ik->pmk/dot_general | solution.py:49
  (7 shorter events, 0.0 us)
Async XLA Ops:
  7.2 90.6 %all-reduce.3.cloned.1.call-start = ((), (), s32[]{:S(2)}) async-start(), calls=%async_computation.2 | async-start | bytes 1048576 | tf_op jit(solution)/shard_map/psum | solution.py:26
  58.8 91.4 %all-gather.3.cloned.1.call-start = ((), (), s32[]{:S(2)}) async-start(), calls=%async_computation.3 | async-start | bytes 4718592 | tf_op jit(solution)/shard_map/all_gather | solution.py:30
  115.5 535.7 %all-reduce.5.cloned.1.call-start = ((), (), s32[]{:S(2)}) async-start(), calls=%async_computation.4 | async-start | bytes 1048576 | tf_op jit(solution)/shard_map/psum | solution.py:26
  168.5 112.5 %copy-start.3 = (f32[1024,1024]{1,0:T(8,128)}, f32[1024,1024]{1,0:T(8,128)S(1)}, u32[]{:S(2)}) copy-start(f32[1024,1024]{1,0:T(8,128)S(1)} %fusion.4) | copy-start | bytes 12582916
  558.7 6.2 copy-start
  612.4 91.3 %all-gather.5.cloned.1.call-start = ((), (), s32[]{:S(2)}) async-start(), calls=%async_computation.5 | async-start | bytes 4718592 | tf_op jit(solution)/shard_map/all_gather | solution.py:30
  722.0 59.2 %copy-start.1 = (f32[1024,1024]{1,0:T(8,128)}, f32[1024,1024]{1,0:T(8,128)S(1)}, u32[]{:S(2)}) copy-start(f32[1024,1024]{1,0:T(8,128)S(1)} %fusion.5) | copy-start | bytes 12582916
  794.2 189.7 %all-to-all-start.1 = ((f32[8,32,128,128]{3,2,1,0:T(8,128)}), f32[8,32,128,128]{3,2,1,0:T(8,128)}, u32[]{:S(2)}, u32[]{:S(2)}) async-start(f32[8,32,128,128]{3,2,1,0:T(8,128)} %fusion.13), calls=%async_computation.1 | async-start | bytes 33554432 | tf_op jit(solution)/shard_map/all_to_all | solution.py:44
  983.9 7.1 copy-start.2
Sparse Core Ops, SparseCore 0:
  58.9 38.7 all-reduce.2
  115.6 34.5 all-gather.2
  612.5 38.6 all-reduce.4
  669.1 34.5 all-gather.4
